TPU v7x, 32 devices: a whole 2x2x4 slice. The times are simulated.
32 devices in a mesh: rep: 8 (over z, x), shard: 4 (over y, core).
Axes of the slice: x: 2, y: 2, z: 4, core: 2. Of those that a mesh axis runs over, the one named last changes fastest.
Arguments:
- inputs: bfloat16 [3072, 1024], P('rep', 'shard'), may hold values from -6 to 6
- cotangent: bfloat16 [3072, 512], P('rep'), may hold values from -0.15625 to 0.15625
- momentum: float32 [512, 1024], P('rep', 'shard'), may hold values from -54 to 54
- right_prev: float32 [1024, 64], P('shard'), may hold values from -0.1875 to 0.1875
Outputs:
- new_momentum: float32 [512, 1024], P('rep', 'shard')
- right_factor: float32 [1024, 64], P('shard')
- update: bfloat16 [512, 1024], P('rep', 'shard')
All inputs are finite; a program needn't handle non-finite values.
Results may differ from a plain program's by a relative error of at most 0.001.
Values sent between devices are 32-bit elements; how exact they have to be, the bound alone decides.
A program may use at most 64 MiB of HBM per device.

v0:
```python
import jax
import jax.numpy as jnp
from jax import lax
from jax.sharding import PartitionSpec as P


def body(inputs, cotangent, momentum, right_prev):
    high = lax.Precision.HIGHEST
    col_count = momentum.shape[1]
    out_total = cotangent.shape[1]
    in_total = col_count * lax.axis_size("shard")
    rank_size = right_prev.shape[1]
    gradient = lax.psum_scatter(
        lax.dot_general(
            cotangent, inputs, (((0,), (0,)), ((), ())), preferred_element_type=jnp.float32
        ),
        "rep",
        scatter_dimension=0,
        tiled=True,
    )
    blended = momentum + gradient
    left_raw = lax.psum(jnp.dot(blended, right_prev, precision=high), "shard")
    gram_sum = lax.psum(jnp.dot(left_raw.T, left_raw, precision=high), "rep")
    lower_factor = jnp.linalg.cholesky(gram_sum)
    ortho = lax.linalg.triangular_solve(lower_factor, left_raw.T, left_side=True, lower=True).T
    local_right = jnp.dot(blended.T, ortho, precision=high)
    right_raw = lax.psum(local_right, "rep")
    column_sq = lax.psum(jnp.sum(right_raw * right_raw, axis=0), "shard")
    new_momentum = blended - 0.05 * jnp.dot(ortho, right_raw.T, precision=high)
    right_factor = right_raw / jnp.sqrt(column_sq + 1e-06)
    scale_factor = (out_total * in_total / rank_size) ** 0.5
    update = (scale_factor * jnp.dot(ortho, right_factor.T, precision=high)).astype(jnp.bfloat16)
    return (new_momentum, right_factor, update)


def solution(mesh):
    return jax.shard_map(
        body,
        mesh=mesh,
        in_specs=(P("rep", "shard"), P("rep", None), P("rep", "shard"), P("shard", None)),
        out_specs=(P("rep", "shard"), P("shard", None), P("rep", "shard")),
        check_vma=False,
    )
```

profile of v0, /device:TPU:0, one launch (start us, length us, event | category | flops | bytes accessed | tf_op | source)
XLA Modules:
  0.0 219.4 jit_solution(16988871786383340574)
XLA Ops:
  7.2 0.0 copy-start
  7.2 0.0 reduce-scatter.2.cloned.1.call-start
  7.2 0.9 copy-done
  8.2 2.1 fusion.6
  10.2 0.0 reduce-scatter.2.cloned.1.call-update
  10.2 0.0 copy-start.4
  10.3 0.0 all-reduce.2.cloned.1.call-start
  10.3 66.9 %reduce-scatter.2.cloned.1.call-done = f32[64,256]{1,0:T(8,128)} async-done(((f32[512,256]{1,0:T(8,128)}), f32[64,256]{1,0:T(8,128)}) %reduce-scatter.2.cloned.1.call-update) | async-done | bytes 65552 | tf_op jit(solution)/shard_map/reduce_scatter | solution.py:13
  77.2 0.0 copy-done.3
  77.2 0.8 add.30
  78.0 0.0 copy-done.4
  78.0 0.2 fusion.7
  78.3 10.3 %psum.28 = f32[64,64]{1,0:T(8,128)S(1)} all-reduce(f32[64,64]{1,0:T(8,128)S(1)} %fusion.7), channel_id=1, replica_groups=mesh['rep'=8,'shard'=4] {'shard'}, use_global_device_ids=true, to_apply=%region_1.0 | all-reduce | flops 4096 | bytes 32768 | tf_op jit(solution)/shard_map/psum | solution.py:22
  88.5 0.2 fusion.8
  88.8 35.1 %psum.29 = f32[64,64]{0,1:T(8,128)S(1)} all-reduce(f32[64,64]{0,1:T(8,128)S(1)} %fusion.8), channel_id=1, replica_groups=mesh['rep'=8,'shard'=4] {'rep'}, use_global_device_ids=true, to_apply=%region_2.0 | all-reduce | flops 4096 | bytes 32768 | tf_op jit(solution)/shard_map/psum | solution.py:23
  123.9 0.1 copy.8
  124.0 5.9 %cholesky.16 = f32[64,64]{1,0:T(8,128)S(1)} custom-call(f32[64,64]{1,0:T(8,128)S(1)} %fusion.5), custom_call_target="Cholesky" | custom-call | tf_op jit(solution)/shard_map/jit(cholesky)/cholesky | solution.py:24
  129.9 0.6 compare_reduce_fusion
  130.5 0.7 fusion.2
  131.2 4.9 %custom-call.6 = f32[1,64,64]{1,2,0:T(8,128)S(1)} custom-call(f32[1,64,64]{2,1,0:T(8,128)S(1)} %fusion.2), custom_call_target="InvertDiagBlocksLowerTriangular" | custom-call | tf_op jit(solution)/shard_map/triangular_solve | solution.py:25
  136.1 0.2 fusion.3
  136.3 0.8 fusion.9
  137.2 0.0 all-reduce.2.cloned.1.call-update
  137.2 66.8 %all-reduce.2.cloned.1.call-done = f32[256,64]{0,1:T(8,128)} async-done(((f32[256,64]{0,1:T(8,128)}), f32[256,64]{0,1:T(8,128)}) %all-reduce.2.cloned.1.call-update) | async-done | bytes 65552 | tf_op jit(solution)/shard_map/psum | solution.py:27
  204.0 1.0 multiply_reduce_fusion
  205.0 5.7 %psum.31 = f32[64]{0:T(128)S(1)} all-reduce(f32[64]{0:T(128)S(1)} %multiply_reduce_fusion), channel_id=1, replica_groups=mesh['rep'=8,'shard'=4] {'shard'}, use_global_device_ids=true, to_apply=%region_7.8 | all-reduce | flops 64 | bytes 512 | tf_op jit(solution)/shard_map/psum | solution.py:28
  210.7 0.0 copy-done.1
  210.7 0.1 broadcast_divide_fusion
  210.8 0.0 copy-start.2
  210.8 0.9 fusion.1
  211.7 0.0 copy-done.2
  211.7 0.9 fusion
  (5 shorter events, 0.1 us)
Async XLA Ops:
  7.2 1.0 copy-start
  7.2 70.0 %reduce-scatter.2.cloned.1.call-start = ((), (), s32[]{:S(2)}) async-start(), calls=%async_computation.1 | async-start | bytes 589824 | tf_op jit(solution)/shard_map/reduce_scatter | solution.py:13
  10.2 67.0 %copy-start.3 = (f32[64,256]{1,0:T(8,128)S(1)}, f32[64,256]{1,0:T(8,128)}, u32[]{:S(2)}) copy-start(f32[64,256]{1,0:T(8,128)} %param.6) | copy-start | bytes 196612
  10.2 67.8 %copy-start.4 = (f32[256,64]{0,1:T(8,128)S(1)}, f32[256,64]{0,1:T(8,128)}, u32[]{:S(2)}) copy-start(f32[256,64]{0,1:T(8,128)} %param.7) | copy-start | bytes 196612
  10.3 193.7 %all-reduce.2.cloned.1.call-start = ((), (), s32[]{:S(2)}) async-start(), calls=%async_computation.2 | async-start | bytes 131072 | tf_op jit(solution)/shard_map/psum | solution.py:27
  204.0 6.7 %copy-start.1 = (f32[256,64]{0,1:T(8,128)S(1)}, f32[256,64]{0,1:T(8,128)}, u32[]{:S(2)}) copy-start(f32[256,64]{0,1:T(8,128)} %all-reduce.2.cloned.1.call-done) | copy-start | bytes 196612
  210.8 0.9 copy-start.2
Sparse Core Ops, SparseCore 0:
  11.3 65.8 reduce-scatter.1
  137.3 66.6 all-reduce.1
where the time goes:
time: 220 us; the launch traced here: 219 us
  waiting for transfers between devices  134 us (61%)
  blocking collectives  51.1 us (23%)
  other arithmetic  14.1 us (6%)
  between operations  14.1 us (6%)
  matrix products  5.31 us (2%)
    reduce_scatter x1, waiting for transfers between devices, body(): lax.psum_scatter(lax.dot_general(cotangent, inputs, (((0,), (0,)), ((), (...  66.9 us
    psum x1, waiting for transfers between devices, body(): right_raw = lax.psum(local_right, 'rep')  66.8 us
    psum x1, blocking collectives, body(): gram_sum = lax.psum(jnp.dot(left_raw.T, left_raw, precision=high), 'rep')  35.1 us
    psum x1, blocking collectives, body(): left_raw = lax.psum(jnp.dot(blended, right_prev, precision=high), 'shard')  10.3 us
    another operation x3, other arithmetic, body(): lower_factor = jnp.linalg.cholesky(gram_sum)  6.53 us
    psum x1, blocking collectives, body(): column_sq = lax.psum(jnp.sum(right_raw * right_raw, axis=0), 'shard')  5.67 us
    another operation x2, other arithmetic, body(): lax.linalg.triangular_solve(lower_factor, left_raw.T, left_side=True, low...  5.57 us
  transfers between devices with their start and end apart: 2, of which 2 were waited for; matrix products, arithmetic and copies ran while one was open for 0% of the time, Pallas kernels for 0%

commit v1 on v0

--- a/solution.py
+++ b/solution.py
@@ -24,7 +24,7 @@
     lower_factor = jnp.linalg.cholesky(gram_sum)
     ortho = lax.linalg.triangular_solve(lower_factor, left_raw.T, left_side=True, lower=True).T
     local_right = jnp.dot(blended.T, ortho, precision=high)
-    right_raw = lax.psum(local_right, "rep")
+    right_raw = jnp.sum(lax.all_gather(local_right, "rep"), axis=0)
     column_sq = lax.psum(jnp.sum(right_raw * right_raw, axis=0), "shard")
     new_momentum = blended - 0.05 * jnp.dot(ortho, right_raw.T, precision=high)
     right_factor = right_raw / jnp.sqrt(column_sq + 1e-06)

time: 220 us -> 183 us (0.83)
  waiting for transfers between devices: 134 us -> 66.9 us
  blocking collectives: 51.1 us -> 82.3 us
    psum x1 -> x0, waiting for transfers between devices: 66.8 us -> none  [body(): right_raw = lax.psum(local_right, 'rep')]
    all_gather x0 -> x1, blocking collectives: none -> 31.3 us  [body(): right_raw = jnp.sum(lax.all_gather(local_right, 'rep'), axis=0)]
  transfers between devices with their start and end apart: 2 -> 1, of which waited for: 2 -> 1; matrix products, arithmetic and copies ran while one was open for 0% -> 0% of each run, Pallas kernels for 0% -> 0%
where the time goes in v1:
time: 183 us
  blocking collectives  82.3 us (45%)
  waiting for transfers between devices  66.9 us (37%)
  between operations  14.1 us (8%)
  other arithmetic  13.3 us (7%)
  matrix products  4.7 us (3%)
    reduce_scatter x1, waiting for transfers between devices, body(): lax.psum_scatter(lax.dot_general(cotangent, inputs, (((0,), (0,)), ((), (...  66.9 us
    psum x1, blocking collectives, body(): gram_sum = lax.psum(jnp.dot(left_raw.T, left_raw, precision=high), 'rep')  35.1 us
    all_gather x1, blocking collectives, body(): right_raw = jnp.sum(lax.all_gather(local_right, 'rep'), axis=0)  31.3 us
    psum x1, blocking collectives, body(): left_raw = lax.psum(jnp.dot(blended, right_prev, precision=high), 'shard')  10.3 us
    another operation x3, other arithmetic, body(): lower_factor = jnp.linalg.cholesky(gram_sum)  6.52 us
    psum x1, blocking collectives, body(): column_sq = lax.psum(jnp.sum(right_raw * right_raw, axis=0), 'shard')  5.67 us
    another operation x2, other arithmetic, body(): lax.linalg.triangular_solve(lower_factor, left_raw.T, left_side=True, low...  5.55 us
  transfers between devices with their start and end apart: 1, of which 1 were waited for; matrix products, arithmetic and copies ran while one was open for 0% of the time, Pallas kernels for 0%

profile of v1, /device:TPU:0, one launch (start us, length us, event | category | flops | bytes accessed | tf_op | source)
XLA Modules:
  0.0 182.6 jit_solution(7999281405163538785)
XLA Ops:
  7.2 0.0 copy-start
  7.2 0.0 reduce-scatter.2.cloned.1.call-start
  7.2 0.9 copy-done
  8.2 2.1 %fusion.6 = f32[512,256]{1,0:T(8,128)} fusion(bf16[384,512]{1,0:T(8,128)(2,1)S(1)} %copy-done, bf16[384,256]{1,0:T(8,128)(2,1)} %param.4), kind=kOutput, calls=%fused_computation.18 | convolution fusion | flops 100663296 | bytes 1114112 | tf_op jit(solution)/shard_map/dot_general | solution.py:14
  10.2 0.0 copy-start.2
  10.2 0.0 reduce-scatter.2.cloned.1.call-update
  10.2 0.0 copy-start.3
  10.3 66.9 %reduce-scatter.2.cloned.1.call-done = f32[64,256]{1,0:T(8,128)} async-done(((f32[512,256]{1,0:T(8,128)}), f32[64,256]{1,0:T(8,128)}) %reduce-scatter.2.cloned.1.call-update) | async-done | bytes 65552 | tf_op jit(solution)/shard_map/reduce_scatter | solution.py:13
  77.2 0.0 copy-done.2
  77.2 0.8 add.28
  78.0 0.0 copy-done.3
  78.0 0.2 fusion.7
  78.3 10.3 %psum.21 = f32[64,64]{1,0:T(8,128)S(1)} all-reduce(f32[64,64]{1,0:T(8,128)S(1)} %fusion.7), channel_id=1, replica_groups=mesh['rep'=8,'shard'=4] {'shard'}, use_global_device_ids=true, to_apply=%region_1.0 | all-reduce | flops 4096 | bytes 32768 | tf_op jit(solution)/shard_map/psum | solution.py:22
  88.5 0.2 fusion.8
  88.8 35.1 %psum.22 = f32[64,64]{0,1:T(8,128)S(1)} all-reduce(f32[64,64]{0,1:T(8,128)S(1)} %fusion.8), channel_id=1, replica_groups=mesh['rep'=8,'shard'=4] {'rep'}, use_global_device_ids=true, to_apply=%region_2.0 | all-reduce | flops 4096 | bytes 32768 | tf_op jit(solution)/shard_map/psum | solution.py:23
  123.9 0.1 copy.8
  124.0 5.8 %cholesky.16 = f32[64,64]{1,0:T(8,128)S(1)} custom-call(f32[64,64]{1,0:T(8,128)S(1)} %fusion.5), custom_call_target="Cholesky" | custom-call | tf_op jit(solution)/shard_map/jit(cholesky)/cholesky | solution.py:24
  129.9 0.6 compare_reduce_fusion
  130.5 0.7 fusion.2
  131.2 4.9 %custom-call.6 = f32[1,64,64]{1,2,0:T(8,128)S(1)} custom-call(f32[1,64,64]{2,1,0:T(8,128)S(1)} %fusion.2), custom_call_target="InvertDiagBlocksLowerTriangular" | custom-call | tf_op jit(solution)/shard_map/triangular_solve | solution.py:25
  136.1 0.2 fusion.3
  136.3 0.2 fusion.9
  136.5 31.3 %all-gather = f32[2048,64]{0,1:T(8,128)S(1)} all-gather(f32[256,64]{0,1:T(8,128)S(1)} %fusion.9), channel_id=2, replica_groups=mesh['rep'=8,'shard'=4] {'rep'}, dimensions={0}, use_global_device_ids=true | all-gather | bytes 589824 | tf_op jit(solution)/shard_map/all_gather | solution.py:27
  167.8 0.2 copy.10
  168.0 0.1 bitcast_reduce_fusion
  168.1 0.9 fusion
  169.0 0.1 multiply_reduce_fusion
  169.1 5.7 %psum.23 = f32[64]{0:T(128)S(1)} all-reduce(f32[64]{0:T(128)S(1)} %multiply_reduce_fusion), channel_id=1, replica_groups=mesh['rep'=8,'shard'=4] {'shard'}, use_global_device_ids=true, to_apply=%region_7.8 | all-reduce | flops 64 | bytes 512 | tf_op jit(solution)/shard_map/psum | solution.py:28
  174.8 0.1 broadcast_divide_fusion
  174.9 0.0 copy-start.1
  174.9 0.9 fusion.1
  175.8 0.0 copy-done.1
  (3 shorter events, 0.0 us)
Async XLA Ops:
  7.2 1.0 copy-start
  7.2 70.0 %reduce-scatter.2.cloned.1.call-start = ((), (), s32[]{:S(2)}) async-start(), calls=%async_computation.1 | async-start | bytes 589824 | tf_op jit(solution)/shard_map/reduce_scatter | solution.py:13
  10.2 67.0 %copy-start.2 = (f32[64,256]{1,0:T(8,128)S(1)}, f32[64,256]{1,0:T(8,128)}, u32[]{:S(2)}) copy-start(f32[64,256]{1,0:T(8,128)} %param.6) | copy-start | bytes 196612
  10.2 67.8 %copy-start.3 = (f32[256,64]{0,1:T(8,128)S(1)}, f32[256,64]{0,1:T(8,128)}, u32[]{:S(2)}) copy-start(f32[256,64]{0,1:T(8,128)} %param.7) | copy-start | bytes 196612
  174.9 0.9 copy-start.1
Sparse Core Ops, SparseCore 0:
  11.3 65.8 reduce-scatter.1
